TPU v7x, 32 devices: a whole 2x2x4 slice. The times are simulated.
32 devices in a mesh: segment: 2 (over core), clip: 4 (over z), tile: 4 (over y, x).
Axes of the slice: x: 2, y: 2, z: 4, core: 2. Of those that a mesh axis runs over, the one named last changes fastest.
Arguments:
- video: bfloat16 [4, 4, 3, 12, 4, 256], P('clip', 'tile'), may hold values from -6 to 6
- cotangent: bfloat16 [4, 4, 3, 12, 4, 256], P('clip', 'tile'), may hold values from -6 to 6
- weights: bfloat16 [2, 27, 256, 256], P('segment'), may hold values from -0.078125 to 0.078125
- neighbours: int32 [4, 4, 2], P('clip', 'tile'), may hold values from 0 to 4, as said below
- rows_used: int32 [4, 4], P('clip', 'tile'), may hold values from 3 to 12, as said below
- cols_used: int32 [4], P('clip'), may hold values from 2 to 4, as said below
Outputs:
- section_out: bfloat16 [2, 4, 4, 3, 12, 4, 256], P('segment', 'clip', 'tile')
- grads: float32 [2, 3, 589824], P('segment', None, ('clip', 'tile'))
Inputs may be any that keep to these rules, and one draw needn't show every extreme that they name: `neighbours`: in each clip the strips of its frames lie on the 4 tiles in an order of their own: entry 0 names the tile of the strip above, entry 1 the tile of the strip below, 4 where there is none; exactly one strip of each clip has none above and one has none below, and the entries chain all 4 strips of a clip top to bottom. `rows_used`: in every clip some strip has 12 rows. `cols_used`: some clip has 4 columns.
All inputs are finite; a program needn't handle non-finite values.
Results may differ from a plain program's by a relative error of at most 0.0054.
Values may be sent and summed in bfloat16 or wider, within the bound.
A program may use at most 576 MiB of HBM per device.

v0:
```python
import jax
import jax.numpy as jnp
from jax import lax
from jax.sharding import PartitionSpec as P


def shifted(block, axis, distance):
    devices = range(lax.axis_size(axis))
    route = [(i - distance, i) for i in devices if i - distance in devices]
    return lax.ppermute(block, axis, route)


def silu_grad(values):
    sigmoid = jax.nn.sigmoid(values)
    return sigmoid * (1.0 + values * (1.0 - sigmoid))


def pad_block(strip_field, upper, bottom, row_count):
    frame_count, height, columns, channels = strip_field.shape
    blank = jnp.zeros((frame_count, 1, columns, channels), strip_field.dtype)
    padded = jnp.concatenate([upper[:, None], strip_field, blank], axis=1)
    padded = lax.dynamic_update_slice_in_dim(padded, bottom[:, None], row_count + 1, axis=1)
    return jnp.pad(padded, ((0, 0), (0, 0), (1, 1), (0, 0)))


def patches(stacked, frame_count, height, columns):
    pieces = []
    for depth_off in range(3):
        for row_off in range(3):
            for col_off in range(3):
                pieces.append(
                    stacked[
                        depth_off : depth_off + frame_count,
                        row_off : row_off + height,
                        col_off : col_off + columns,
                    ]
                )
    return jnp.concatenate(pieces, axis=-1).reshape(frame_count * height * columns, -1)


def every_tap_entries(patch_fwd, weighting, start, count, channels):
    span = 9 * channels
    row_total = min(count // channels + 2, span)
    row_low = jnp.minimum(start // channels, span - row_total)
    columns = jnp.concatenate(
        [
            lax.dynamic_slice_in_dim(patch_fwd, tap * span + row_low, row_total, 1)
            for tap in range(3)
        ],
        axis=1,
    )
    contract = (((0,), (0,)), ((), ()))
    block = lax.dot_general(
        columns, weighting, contract, preferred_element_type=jnp.float32
    ).reshape(3, -1)
    return block.T


def local(video, cotangent, weights, neighbours, rows_used, cols_used):
    window = video[0, 0]
    frame_count, height, columns, channels = window.shape
    tile_count = lax.axis_size("tile")
    section = lax.axis_index("segment")
    row_count = rows_used[0, 0]
    col_count = cols_used[0]
    upper_tile = neighbours[0, 0, 0]
    lower_tile = neighbours[0, 0, 1]
    row_ids = jnp.arange(height, dtype=jnp.int32)
    col_ids = jnp.arange(columns, dtype=jnp.int32)
    inside = (row_ids[:, None] < row_count) & (col_ids[None, :] < col_count)
    inside_mask = inside[None, :, :, None]
    kernel = weights[0]
    forward_mat = kernel.reshape(27 * channels, channels)
    backward_mat = kernel[::-1].transpose(0, 2, 1).reshape(27 * channels, channels)
    front_zero = jnp.zeros((2, height + 2, columns + 2, channels), jnp.bfloat16)

    def halo_block(field):
        leading = field[:, 0]
        trailing = lax.dynamic_index_in_dim(field, row_count - 1, axis=1, keepdims=False)
        both_rows = jnp.stack([leading, trailing], axis=1)
        gathered = lax.all_gather(both_rows[None], "tile", axis=0, tiled=True)
        upper = gathered[jnp.minimum(upper_tile, tile_count - 1), :, 1]
        bottom = gathered[jnp.minimum(lower_tile, tile_count - 1), :, 0]
        upper = jnp.where(upper_tile < tile_count, upper, jnp.zeros_like(upper))
        bottom = jnp.where(lower_tile < tile_count, bottom, jnp.zeros_like(bottom))
        return pad_block(field, upper, bottom, row_count)

    def advance(entry, history):
        count = entry.shape[0]
        activated = jax.nn.silu(entry.astype(jnp.float32)).astype(jnp.bfloat16)
        padded = halo_block(activated)
        stacked = jnp.concatenate([history, padded], axis=0)
        mixed = jnp.dot(
            patches(stacked, count, height, columns),
            forward_mat,
            preferred_element_type=jnp.float32,
        ).reshape(entry.shape)
        result = jnp.where(inside_mask, entry.astype(jnp.float32) + mixed, 0.0).astype(jnp.bfloat16)
        return (result, stacked[-2:], padded)

    source = jnp.where(inside_mask, window, jnp.zeros_like(window))
    is_encoder = section == 0
    first_out, first_hist, first_pad = advance(source, front_zero)
    latent = shifted(first_out, "segment", 1)
    second_out, second_hist, second_pad = advance(latent, front_zero)
    own_out = jnp.where(is_encoder, first_out, second_out)
    own_input = jnp.where(is_encoder, source, latent)
    own_pad = jnp.where(is_encoder, first_pad, second_pad)
    target = jnp.where(inside_mask, cotangent[0, 0], jnp.zeros_like(cotangent[0, 0]))
    patch_fwd = patches(
        jnp.concatenate([front_zero, own_pad], axis=0), frame_count, height, columns
    )
    back_stack = jnp.concatenate([halo_block(target), front_zero], axis=0)
    spread = jnp.dot(
        patches(back_stack, frame_count, height, columns),
        backward_mat,
        preferred_element_type=jnp.float32,
    ).reshape(target.shape)
    own_grad = jnp.where(
        inside_mask,
        target.astype(jnp.float32) + silu_grad(own_input.astype(jnp.float32)) * spread,
        0.0,
    ).astype(jnp.bfloat16)
    returned = shifted(own_grad, "segment", -1)
    weighting = jnp.where(is_encoder, returned, target).reshape(-1, channels)
    flat_rows = 9 * channels * channels // lax.axis_size(("clip", "tile"))
    shares = lax.psum_scatter(
        every_tap_entries(
            patch_fwd,
            weighting,
            jnp.int32(0),
            flat_rows * lax.axis_size(("clip", "tile")),
            channels,
        ),
        ("clip", "tile"),
        scatter_dimension=0,
        tiled=True,
    )
    summed = shares.T
    return (own_out[None, None, None], summed[None])


def solution(mesh):
    in_specs = (
        P("clip", "tile", None, None, None, None),
        P("clip", "tile", None, None, None, None),
        P("segment", None, None, None),
        P("clip", "tile", None),
        P("clip", "tile"),
        P("clip"),
    )
    out_specs = (
        P("segment", "clip", "tile", None, None, None, None),
        P("segment", None, ("clip", "tile")),
    )
    return jax.shard_map(local, mesh=mesh, in_specs=in_specs, out_specs=out_specs, check_vma=False)
```

profile of v0, /device:TPU:0, one launch (start us, length us, event | category | flops | bytes accessed | tf_op | source)
XLA Modules:
  0.0 367.3 jit_solution(6660135488782941422)
XLA Ops:
  7.2 0.0 all-reduce.10.cloned.1.call-start
  7.2 1.3 fusion.28
  12.4 0.1 broadcast_and_fusion
  12.5 1.0 bitcast_select_fusion
  13.5 1.0 fusion.18
  14.6 9.7 %all-gather.2 = bf16[12,2,4,256]{3,2,1,0:T(4,128)(2,1)S(1)} all-gather(bf16[3,2,4,256]{3,2,1,0:T(4,128)(2,1)S(1)} %copy.127), channel_id=4, replica_groups=mesh['segment'=2,'clip'=4,'tile'=4] {'tile'}, dimensions={0}, use_global_device_ids=true | all-gather | bytes 61440 | tf_op jit(solution)/shard_map/all_gather | solution.py:81
  24.4 8.2 %all-gather = bf16[12,2,4,256]{3,2,1,0:T(4,128)(2,1)S(1)} all-gather(bf16[3,2,4,256]{3,2,1,0:T(4,128)(2,1)S(1)} %copy.120), channel_id=2, replica_groups=mesh['segment'=2,'clip'=4,'tile'=4] {'tile'}, dimensions={0}, use_global_device_ids=true | all-gather | bytes 61440 | tf_op jit(solution)/shard_map/all_gather | solution.py:81
  32.7 0.1 pad.29.clone
  32.8 0.1 maximum_maximum_fusion.2
  32.9 0.1 dynamic_update_slice.9
  33.7 1.4 copy-done
  35.0 0.9 fusion.2
  35.9 1.3 collective-permute-start
  37.2 0.1 dynamic_update_slice.11
  37.4 5.7 %copy.130 = bf16[1,27,256,256]{2,3,1,0:T(8,128)(2,1)} copy(bf16[1,27,256,256]{3,2,1,0:T(8,128)(2,1)} %param.8) | data formatting | bytes 7077888 | tf_op args[2]
  43.7 4.2 %rev.3 = bf16[27,256,256]{1,2,0:T(8,128)(2,1)} reverse(bf16[27,256,256]{1,2,0:T(8,128)(2,1)} %bitcast.80), dimensions={0} | reverse | bytes 7077888 | tf_op jit(solution)/shard_map/rev | solution.py:74
  48.0 3.0 fusion.14
  51.0 7.3 %all-gather.1 = bf16[12,2,4,256]{3,2,1,0:T(4,128)(2,1)S(1)} all-gather(bf16[3,2,4,256]{3,2,1,0:T(4,128)(2,1)S(1)} %copy.123), channel_id=3, replica_groups=mesh['segment'=2,'clip'=4,'tile'=4] {'tile'}, dimensions={0}, use_global_device_ids=true | all-gather | bytes 61440 | tf_op jit(solution)/shard_map/all_gather | solution.py:81
  58.3 0.1 maximum_maximum_fusion.1
  58.4 0.1 dynamic_update_slice.10
  59.2 1.5 collective-permute-start.1
  60.7 1.7 collective-permute-done.1
  62.4 4.0 %convolution_bitcast_fusion = f32[6912,256]{1,0:T(8,128)} fusion(bf16[3,12,4,6912]{3,1,2,0:T(8,128)(2,1)S(1)} %constant_dynamic-update-slice_fusion.54, bf16[3,12,4,256]{3,1,2,0:T(8,128)(2,1)S(1)} %collective-permute-done.1, pred[]{:T(512)S(6)} %eq.3, bf16[1,1,3,12,4,256]{5,4,3,2,1,0:T(4,128)(2,1)S(1)} %copy-done.3, pred[12,4]{0,1:T(4,128)(4,1)S(1)} %broadcast_and_fusion), kind=kOutput, calls=%fused_computation | convolution fusion | flops 509681664 | bytes 9216049 | tf_op jit(solution)/shard_map/dot_general | solution.py:53
  66.4 10.6 %reshape.152 = f32[3,589824]{1,0:T(4,128)} reshape(f32[6912,256]{1,0:T(8,128)} %convolution_bitcast_fusion) | data formatting | bytes 14155776 | tf_op jit(solution)/shard_map/reshape | solution.py:55
  77.0 0.6 copy-done.4
  77.6 0.6 dynamic-slice
  79.5 1.4 copy-done.1
  80.9 0.9 fusion.5
  81.8 0.7 copy.131
  82.5 275.6 %all-reduce.10.cloned.1.call-done = f32[589824,3]{0,1:T(4,128)} async-done(((f32[589824,3]{0,1:T(4,128)}), f32[589824,3]{0,1:T(4,128)}) %all-reduce.10.cloned.1.call-update) | async-done | bytes 7077904
  358.1 1.2 dynamic-slice_bitcast_fusion
  359.2 1.2 copy.132
  (139 shorter events, 2.2 us)
Async XLA Ops:
  7.2 350.9 %all-reduce.10.cloned.1.call-start = ((), (), s32[]{:S(2)}) async-start(), calls=%async_computation | async-start | bytes 18874368
  33.0 2.0 copy-start
  33.1 2.0 copy-start.2
  35.9 12.0 %collective-permute-start = (bf16[3,12,4,256]{3,1,2,0:T(8,128)(2,1)S(1)}, bf16[3,12,4,256]{3,1,2,0:T(8,128)(2,1)S(1)}, u32[]{:S(2)}, u32[]{:S(2)}) collective-permute-start(bf16[3,12,4,256]{3,1,2,0:T(8,128)(2,1)S(1)} %fusion.2), channel_id=1, source_target_pairs={{0,16},{1,17},{2,18},{3,19},{4,20},{5,21},{6,22},{7,23},{8,24},{9,... | collective-permute-start | bytes 221192 | tf_op jit(solution)/shard_map/ppermute | solution.py:10
  43.7 4.2 %copy-start.3 = (bf16[1,1,3,12,4,256]{5,4,3,2,1,0:T(4,128)(2,1)S(1)}, bf16[1,1,3,12,4,256]{5,4,3,2,1,0:T(4,128)(2,1)}, u32[]{:S(2)}) copy-start(bf16[1,1,3,12,4,256]{5,4,3,2,1,0:T(4,128)(2,1)} %param.7) | copy-start | bytes 221188
  59.2 3.2 collective-permute-start.1
  77.0 0.7 copy-start.4
  78.9 2.0 copy-start.1
Sparse Core Ops, SparseCore 0:
  77.1 280.8 all-reduce.9
where the time goes:
time: 368 us; the launch traced here: 367 us
  waiting for transfers between devices  277 us (75%)
  local copies, waits for them, and re-layouts  31.2 us (8%)
  blocking collectives  25.2 us (7%)
  between operations  19.7 us (5%)
  matrix products  8.71 us (2%)
    unnamed x2, waiting for transfers between devices  276 us
    all_gather x3, blocking collectives, halo_block(): gathered = lax.all_gather(both_rows[None], 'tile', axis=0, tiled=True)  25.2 us
    unnamed x118, local copies, waits for them, and re-layouts  13.4 us
    reshape x1, local copies, waits for them, and re-layouts, every_tap_entries(): block = lax.dot_general(columns, weighting, contract, preferred_element_t...  10.6 us
  transfers between devices with their start and end apart: 3, of which 2 were waited for; matrix products, arithmetic and copies ran while one was open for 4% of the time, Pallas kernels for 0%

commit v1 on v0

--- a/solution.py
+++ b/solution.py
@@ -78,7 +78,10 @@
         leading = field[:, 0]
         trailing = lax.dynamic_index_in_dim(field, row_count - 1, axis=1, keepdims=False)
         both_rows = jnp.stack([leading, trailing], axis=1)
-        gathered = lax.all_gather(both_rows[None], "tile", axis=0, tiled=True)
+        gathered = jnp.concatenate(
+            lax.all_to_all(jnp.stack([both_rows[None]] * lax.axis_size("tile")), "tile", 0, 0),
+            axis=0,
+        )
         upper = gathered[jnp.minimum(upper_tile, tile_count - 1), :, 1]
         bottom = gathered[jnp.minimum(lower_tile, tile_count - 1), :, 0]
         upper = jnp.where(upper_tile < tile_count, upper, jnp.zeros_like(upper))

time: 368 us -> 361 us (0.981)
  blocking collectives: 25.2 us -> 0 us
  starting transfers between devices: 2.81 us -> 15.3 us
  waiting for transfers between devices: 277 us -> 283 us
    all_gather x3 -> x0, blocking collectives: 25.2 us -> none  [halo_block(): gathered = lax.all_gather(both_rows[None], 'tile', axis=0, tiled=True)]
    all_to_all x0 -> x3, starting transfers between devices: none -> 12.6 us  [halo_block(): lax.all_to_all(jnp.stack([both_rows[None]] * lax.axis_size('tile')), 'til...]
    all_to_all x0 -> x3, waiting for transfers between devices: none -> 7.47 us  [halo_block(): lax.all_to_all(jnp.stack([both_rows[None]] * lax.axis_size('tile')), 'til...]
    unnamed x118 -> x124, local copies, waits for them, and re-layouts: 13.4 us -> 13.3 us
  transfers between devices with their start and end apart: 3 -> 6, of which waited for: 2 -> 4; matrix products, arithmetic and copies ran while one was open for 4% -> 3% of each run, Pallas kernels for 0% -> 0%
where the time goes in v1:
time: 361 us; the launch traced here: 360 us
  waiting for transfers between devices  283 us (78%)
  local copies, waits for them, and re-layouts  31.1 us (9%)
  between operations  19.9 us (6%)
  starting transfers between devices  15.3 us (4%)
  matrix products  6.76 us (2%)
  other arithmetic  4.14 us (1%)
    unnamed x2, waiting for transfers between devices  275 us
    unnamed x124, local copies, waits for them, and re-layouts  13.3 us
    all_to_all x3, starting transfers between devices, halo_block(): lax.all_to_all(jnp.stack([both_rows[None]] * lax.axis_size('tile')), 'til...  12.6 us
    reshape x1, local copies, waits for them, and re-layouts, every_tap_entries(): block = lax.dot_general(columns, weighting, contract, preferred_element_t...  10.6 us
    all_to_all x3, waiting for transfers between devices, halo_block(): lax.all_to_all(jnp.stack([both_rows[None]] * lax.axis_size('tile')), 'til...  7.47 us
  transfers between devices with their start and end apart: 6, of which 4 were waited for; matrix products, arithmetic and copies ran while one was open for 3% of the time, Pallas kernels for 0%

profile of v1, /device:TPU:0, one launch (start us, length us, event | category | flops | bytes accessed | tf_op | source)
XLA Modules:
  0.0 359.8 jit_solution(14360478803120073272)
XLA Ops:
  8.6 1.0 bitcast_select_fusion
  9.5 1.1 fusion.18
  10.7 0.6 stack.26
  11.4 5.2 %all-to-all-start.2 = ((bf16[4,1,3,2,4,256]{5,4,2,3,1,0:T(4,128)(2,1)}), bf16[4,1,3,2,4,256]{5,4,2,3,1,0:T(4,128)(2,1)}, u32[]{:S(2)}, u32[]{:S(2)}) async-start(bf16[4,1,3,2,4,256]{5,4,2,3,1,0:T(4,128)(2,1)} %stack.26), calls=%async_computation.2 | async-start | bytes 98304 | tf_op jit(solution)/shard_map/all_to_all | solution.py:82
  16.6 1.4 fusion.28
  20.8 4.4 %copy.103 = bf16[1,27,256,256]{2,3,1,0:T(8,128)(2,1)S(1)} copy(bf16[1,27,256,256]{3,2,1,0:T(8,128)(2,1)} %param.8) | data formatting | bytes 7077888 | tf_op args[2]
  25.2 2.0 rev.3
  27.3 0.6 stack.22
  27.9 4.2 %all-to-all-start = ((bf16[4,1,3,2,4,256]{5,4,2,3,1,0:T(4,128)(2,1)}), bf16[4,1,3,2,4,256]{5,4,2,3,1,0:T(4,128)(2,1)S(1)}, u32[]{:S(2)}, u32[]{:S(2)}) async-start(bf16[4,1,3,2,4,256]{5,4,2,3,1,0:T(4,128)(2,1)} %stack.22), calls=%async_computation | async-start | bytes 98304 | tf_op jit(solution)/shard_map/all_to_all | solution.py:82
  32.1 0.7 select_bitcast_fusion
  32.9 4.0 %all-to-all-done = bf16[4,1,3,2,4,256]{5,4,2,3,1,0:T(4,128)(2,1)S(1)} async-done(((bf16[4,1,3,2,4,256]{5,4,2,3,1,0:T(4,128)(2,1)}), bf16[4,1,3,2,4,256]{5,4,2,3,1,0:T(4,128)(2,1)S(1)}, u32[]{:S(2)}, u32[]{:S(2)}) %all-to-all-start) | async-done | bytes 49184 | tf_op jit(solution)/shard_map/all_to_all | solution.py:82
  37.0 1.1 maximum_maximum_fusion.2
  39.0 1.4 copy-done
  40.3 0.9 fusion.2
  41.2 1.3 collective-permute-start
  43.2 0.3 collective-permute-done
  43.5 1.2 copy-done.2
  44.6 1.0 fusion.14
  45.7 0.6 stack.24
  46.3 3.3 all-to-all-start.1
  49.7 1.3 collective-permute-start.1
  51.0 3.4 all-to-all-done.1
  55.5 4.0 %convolution_bitcast_fusion = f32[6912,256]{1,0:T(8,128)} fusion(bf16[3,12,4,6912]{3,1,2,0:T(8,128)(2,1)S(1)} %constant_dynamic-update-slice_fusion.54, bf16[3,12,4,256]{3,1,2,0:T(8,128)(2,1)S(1)} %collective-permute-done.1, pred[]{:T(512)S(6)} %eq.3, bf16[1,1,3,12,4,256]{5,4,3,2,1,0:T(4,128)(2,1)S(1)} %copy-done.6, pred[12,4]{0,1:T(4,128)(4,1)S(1)} %broadcast_and_fusion), kind=kOutput, calls=%fused_computation | convolution fusion | flops 509681664 | bytes 9216049 | tf_op jit(solution)/shard_map/dot_general | solution.py:53
  59.5 10.6 %reshape.173 = f32[3,589824]{1,0:T(4,128)} reshape(f32[6912,256]{1,0:T(8,128)} %convolution_bitcast_fusion) | data formatting | bytes 14155776 | tf_op jit(solution)/shard_map/reshape | solution.py:55
  70.2 0.6 copy-done.7
  70.8 0.6 dynamic-slice.6
  72.7 1.4 copy-done.1
  74.1 0.9 fusion.5
  75.0 0.7 copy.104
  75.7 274.9 %all-reduce.10.cloned.1.call-done = f32[589824,3]{0,1:T(4,128)} async-done(((f32[589824,3]{0,1:T(4,128)}), f32[589824,3]{0,1:T(4,128)}) %all-reduce.10.cloned.1.call-update) | async-done | bytes 7077904
  350.6 1.2 dynamic-slice_bitcast_fusion
  351.7 1.2 copy.105
  (151 shorter events, 2.9 us)
Async XLA Ops:
  9.5 11.2 %copy-start.3 = (bf16[3,12,4,256]{3,1,2,0:T(8,128)(2,1)}, bf16[3,12,4,256]{3,1,2,0:T(8,128)(2,1)S(1)}, u32[]{:S(2)}) copy-start(bf16[3,12,4,256]{3,1,2,0:T(8,128)(2,1)S(1)} %bitcast_select_fusion) | copy-start | bytes 221188
  10.6 10.2 %copy-start.4 = (bf16[3,12,4,256]{3,1,2,0:T(8,128)(2,1)}, bf16[3,12,4,256]{3,1,2,0:T(8,128)(2,1)S(1)}, u32[]{:S(2)}) copy-start(bf16[3,12,4,256]{3,1,2,0:T(8,128)(2,1)S(1)} %fusion.18) | copy-start | bytes 221188
  11.4 15.9 %all-to-all-start.2 = ((bf16[4,1,3,2,4,256]{5,4,2,3,1,0:T(4,128)(2,1)}), bf16[4,1,3,2,4,256]{5,4,2,3,1,0:T(4,128)(2,1)}, u32[]{:S(2)}, u32[]{:S(2)}) async-start(bf16[4,1,3,2,4,256]{5,4,2,3,1,0:T(4,128)(2,1)} %stack.26), calls=%async_computation.2 | async-start | bytes 98304 | tf_op jit(solution)/shard_map/all_to_all | solution.py:82
  27.9 9.0 %all-to-all-start = ((bf16[4,1,3,2,4,256]{5,4,2,3,1,0:T(4,128)(2,1)}), bf16[4,1,3,2,4,256]{5,4,2,3,1,0:T(4,128)(2,1)S(1)}, u32[]{:S(2)}, u32[]{:S(2)}) async-start(bf16[4,1,3,2,4,256]{5,4,2,3,1,0:T(4,128)(2,1)} %stack.22), calls=%async_computation | async-start | bytes 98304 | tf_op jit(solution)/shard_map/all_to_all | solution.py:82
  38.3 2.0 copy-start
  38.3 2.0 copy-start.5
  41.2 2.2 collective-permute-start
  42.6 2.0 copy-start.2
  42.6 2.0 copy-start.6
  46.3 8.1 %all-to-all-start.1 = ((bf16[4,1,3,2,4,256]{5,4,2,3,1,0:T(4,128)(2,1)}), bf16[4,1,3,2,4,256]{5,4,2,3,1,0:T(4,128)(2,1)S(1)}, u32[]{:S(2)}, u32[]{:S(2)}) async-start(bf16[4,1,3,2,4,256]{5,4,2,3,1,0:T(4,128)(2,1)} %stack.24), calls=%async_computation.1 | async-start | bytes 98304 | tf_op jit(solution)/shard_map/all_to_all | solution.py:82
  49.6 301.0 %all-reduce.10.cloned.1.call-start = ((), (), s32[]{:S(2)}) async-start(), calls=%async_computation.3 | async-start | bytes 18874368
  49.7 5.8 %collective-permute-start.1 = (bf16[3,12,4,256]{3,1,2,0:T(8,128)(2,1)S(1)}, bf16[3,12,4,256]{3,1,2,0:T(8,128)(2,1)S(1)}, u32[]{:S(2)}, u32[]{:S(2)}) collective-permute-start(bf16[3,12,4,256]{3,1,2,0:T(8,128)(2,1)S(1)} %get-tuple-element.18), channel_id=1, source_target_pairs={{16,0},{17,1},{18,2},{19,3},{20,4},{21,5},{22,6},{23,7},{24,8},{25... | collective-permute-start | bytes 221192 | tf_op jit(solution)/shard_map/ppermute | solution.py:10
  70.2 0.7 copy-start.7
  72.1 2.0 copy-start.1
Sparse Core Ops, SparseCore 0:
  70.3 280.2 all-reduce.9
